TPU v7x, 32 devices: a whole 2x2x4 slice. The times are simulated.
32 devices in a mesh: region: 16 (over z, y, x), tm: 2 (over core).
Axes of the slice: x: 2, y: 2, z: 4, core: 2. Of those that a mesh axis runs over, the one named last changes fastest.
Arguments:
- latents: bfloat16 [16, 256, 768], P('region', 'tm')
- output_grad: bfloat16 [16, 256, 768], P('region', 'tm'), may hold values from -6 to 6
- conv_kernel: float32 [4, 768], replicated, may hold values from -1 to 1
- w_query: bfloat16 [768, 768], replicated, may hold values from -0.21875 to 0.21875
- w_key: bfloat16 [768, 768], replicated, may hold values from -0.21875 to 0.21875
- w_value: bfloat16 [768, 768], replicated, may hold values from -0.21875 to 0.21875
- w_out: bfloat16 [768, 768], replicated, may hold values from -0.21875 to 0.21875
- live_counts: int32 [16, 2], P('region', 'tm'), may hold values from 1 to 128, as said below
Outputs:
- input_grad: bfloat16 [16, 256, 768], P('region', 'tm')
Inputs may be any that keep to these rules, and one draw needn't show every extreme that they name: The first live_counts[r, c] of the 128 tokens of region r in span c are valid.
All inputs are finite; a program needn't handle non-finite values.
Results may differ from a plain program's by a relative error of at most 0.018.
The roundings to bfloat16 on the way count: a program that leaves them out, or rounds other values in their place, can miss the bound.
Values may be sent and summed in bfloat16 or wider, within the bound.
A program may use at most 128 MiB of HBM per device.

v0:
```python
import functools
import math

import jax
import jax.numpy as jnp
from jax import lax
from jax.experimental import pallas as pl
from jax.experimental.pallas import tpu as pltpu
from jax.sharding import PartitionSpec as P

H = 12
KW = 4
BLK = 256
KBLK = 1024
NEG = -1e30
bf16 = jnp.bfloat16
f32 = jnp.float32
VM = pl.BlockSpec(memory_space=pltpu.VMEM)
SM = pl.BlockSpec(memory_space=pltpu.SMEM)
ANY = pl.BlockSpec(memory_space=pl.ANY)
MESH = pl.DeviceIdType.MESH


def dot(a, b):
    return jnp.dot(a, b, preferred_element_type=f32)


def dot_t(a, b):
    return lax.dot_general(a, b, (((1,), (1,)), ((), ())), preferred_element_type=f32)


def owner(h, n_reg):
    return (h * n_reg) // H


def head_of(me, n_reg):
    h = (me * H + n_reg - 1) // n_reg
    return h, jnp.logical_and(h < H, owner(h, n_reg) == me)


def greet(barrier, **where):
    pl.semaphore_signal(barrier, inc=1, device_id=where, device_id_type=MESH)


def spread_kernel(
    n_reg, n_tm, lat_ref, og_ref, ck_ref, cnt_ref, wq_ref, wk_ref, wv_ref, wo_ref,
    out_ref, cout_ref,
    wbuf, ext, edge, send, csend, wsem, esem, ssem, rsem, lsem,
):
    me = lax.axis_index("region")
    mt = lax.axis_index("tm")
    t, d = lat_ref.shape[1], lat_ref.shape[2]
    hd = d // H
    loads = [
        pltpu.make_async_copy(ref, wbuf.at[i], wsem.at[i])
        for i, ref in enumerate((wo_ref, wq_ref, wk_ref, wv_ref))
    ]
    for load in loads:
        load.start()
    barrier = pltpu.get_barrier_semaphore()
    _, is_head = head_of(me, n_reg)

    @pl.when(is_head)
    def _():
        for k in range(1, n_reg):
            greet(barrier, region=lax.rem(me + k, n_reg))

    @pl.when(mt > 0)
    def _():
        greet(barrier, tm=jnp.maximum(mt - 1, 0))

    count = cnt_ref[0, 0]
    csend[...] = jnp.zeros(csend.shape, jnp.int32) + count
    ext[0:8, :] = jnp.zeros((8, d), f32)
    ext[8 : 8 + t, :] = lat_ref[0].astype(f32)
    loads[0].wait()
    live = lax.broadcasted_iota(jnp.int32, (t, 1), 0) < count
    g = dot_t(og_ref[0], wbuf[0])
    g = jnp.where(live, g, 0.0).astype(bf16)
    for h in range(H):
        send[h, :, 3 * hd : 4 * hd] = g[:, h * hd : (h + 1) * hd]

    def project(rows, first):
        hidden = ck_ref[0:1, :] * ext[8 : 8 + rows, :]
        for j in range(1, KW):
            hidden = hidden + ck_ref[j : j + 1, :] * ext[8 - j : 8 - j + rows, :]
        hidden = hidden.astype(bf16)
        for i in range(3):
            if first:
                loads[i + 1].wait()
            x = dot(hidden, wbuf[i + 1]).astype(bf16)
            for h in range(H):
                send[h, 0:rows, i * hd : (i + 1) * hd] = x[:, h * hd : (h + 1) * hd]

    project(t, True)
    heads = H - jnp.where(is_head, 1, 0)
    pl.semaphore_wait(barrier, heads + jnp.minimum(n_tm - 1 - mt, 1))
    to_next = pltpu.make_async_remote_copy(
        src_ref=lat_ref.at[0, pl.ds(t - 16, 16)],
        dst_ref=edge,
        send_sem=esem.at[0],
        recv_sem=esem.at[1],
        device_id={"tm": jnp.minimum(mt + 1, n_tm - 1)},
        device_id_type=MESH,
    )

    @pl.when(mt < n_tm - 1)
    def _():
        to_next.start()

    parts = (pl.ds(16, t - 16), pl.ds(0, 16))

    def target_of(i):
        h = lax.rem(me + i, H)
        return h, owner(h, n_reg)

    def away(i, part):
        h, target = target_of(i)
        return pltpu.make_async_remote_copy(
            src_ref=send.at[h, parts[part]],
            dst_ref=out_ref.at[me, parts[part]],
            send_sem=ssem.at[part, i],
            recv_sem=rsem.at[part, me],
            device_id={"region": target},
            device_id_type=MESH,
        )

    def tell(i):
        return pltpu.make_async_remote_copy(
            src_ref=csend,
            dst_ref=cout_ref.at[me],
            send_sem=ssem.at[2, i],
            recv_sem=rsem.at[2, me],
            device_id={"region": target_of(i)[1]},
            device_id_type=MESH,
        )

    head = jnp.minimum(head_of(me, n_reg)[0], H - 1)
    here = pltpu.make_async_copy(send.at[head], out_ref.at[me], lsem.at[0])
    tell_here = pltpu.make_async_copy(csend, cout_ref.at[me], lsem.at[1])

    for i in range(H):

        @pl.when(target_of(i)[1] != me)
        def _():
            away(i, 0).start()

    @pl.when(mt > 0)
    def _():
        to_next.wait_recv()
        ext[0:8, :] = edge[8:16, :].astype(f32)
        project(16, False)

    for i in range(H):

        @pl.when(target_of(i)[1] != me)
        def _():
            tell(i).start()
            away(i, 1).start()

    @pl.when(is_head)
    def _():
        tell_here.start()
        here.start()
        tell_here.wait()
        here.wait()

    for i in range(H):

        @pl.when(target_of(i)[1] != me)
        def _():
            away(i, 0).wait_send()
            away(i, 1).wait_send()
            tell(i).wait_send()

    @pl.when(mt < n_tm - 1)
    def _():
        to_next.wait_send()

    @pl.when(is_head)
    def _():
        for k in range(1, n_reg):
            s = lax.rem(me + k, n_reg)
            pltpu.make_async_copy(csend, cout_ref.at[s], rsem.at[2, s]).wait()
            for i, rows in enumerate(parts):
                pltpu.make_async_copy(send.at[0, rows], out_ref.at[s, rows], rsem.at[i, s]).wait()


def attend_kernel(
    n_reg, hd, chunk_ref, cnt_ref, out_ref, qk, ka, vg, kt, qt, gt, qg, sbuf, wbuf, dkv, dqp
):
    me = lax.axis_index("region")
    t = chunk_ref.shape[1]
    inv_root = 1.0 / math.sqrt(hd)
    _, is_head = head_of(me, n_reg)
    width = 2 * hd
    subs = KBLK // BLK

    def lane(rows):
        return lax.broadcasted_iota(jnp.int32, (rows, width), 1)

    @pl.when(is_head)
    def _():
        def pack(r, off):
            off = pl.multiple_of(off, 16)
            count = cnt_ref[r, 0, 0]
            a = chunk_ref[r, :, 0:width]
            dead = lax.broadcasted_iota(jnp.int32, (t, width), 0) >= count
            bias = jnp.where(jnp.logical_and(lane(t) == 0, dead), NEG, 0.0)
            qk[pl.ds(off, t), :] = a
            ka[pl.ds(off, t), :] = jnp.where(lane(t) < hd, bias, a.astype(f32)).astype(bf16)
            vg[pl.ds(off, t), :] = chunk_ref[r, :, width : 2 * width]
            return off + (count + 15) // 16 * 16

        total = pl.multiple_of(lax.fori_loop(0, n_reg, pack, 0, unroll=4), 16)
        blank = jnp.zeros((KBLK, width), bf16)
        qk[pl.ds(total, KBLK), :] = blank
        ka[pl.ds(total, KBLK), :] = jnp.where(lane(KBLK) == 0, NEG, 0.0).astype(bf16)
        vg[pl.ds(total, KBLK), :] = blank
        blocks = (total + BLK - 1) // BLK
        supers = (total + KBLK - 1) // KBLK

        def ready(i, c):
            at = pl.multiple_of(i * BLK, BLK)
            a = qk[pl.ds(at, BLK), :]
            b = vg[pl.ds(at, BLK), :]
            a_t = a.T
            scaled = (a_t[0:hd, :].astype(f32) * inv_root).astype(bf16)
            one = jnp.where(lax.broadcasted_iota(jnp.int32, (hd, BLK), 0) == 0, 1.0, 0.0)
            qt[i] = jnp.concatenate([one.astype(bf16), scaled], axis=0)
            kt[i] = a_t[hd:, :]
            gt[i] = jnp.concatenate([b.T[hd:, :], jnp.zeros((hd, BLK), bf16)], axis=0)
            low = lane(BLK) < hd
            qg[i, 0:BLK, :] = jnp.where(low, a.astype(f32) * inv_root, 0.0).astype(bf16)
            qg[i, BLK:, :] = jnp.where(low, 0.0, b.astype(f32)).astype(bf16)
            dkv[pl.ds(at, BLK), :] = jnp.zeros((BLK, width), f32)
            return c

        lax.fori_loop(0, supers * subs, ready, 0)

        def fold(x, op):
            return op(x.reshape(BLK // 8, 8, BLK), axis=0)

        def per_queries(qi, c):
            at = pl.multiple_of(qi * BLK, BLK)
            qat, gat = qt[qi], gt[qi]

            def first(ki, m):
                for u in range(subs):
                    kat = pl.multiple_of(ki * KBLK + u * BLK, BLK)
                    s = dot(ka[pl.ds(kat, BLK), :], qat)
                    wbuf[ki * subs + u] = dot(vg[pl.ds(kat, BLK), :], gat)
                    sbuf[ki * subs + u] = s
                    m = jnp.maximum(m, fold(s, jnp.max))
                return m

            m = lax.fori_loop(0, supers, first, jnp.full((8, BLK), NEG, f32))
            m = jnp.max(m, axis=0, keepdims=True)

            def middle(ki, carry):
                l, dl = carry
                for u in range(subs):
                    p = jnp.exp(sbuf[ki * subs + u] - m)
                    sbuf[ki * subs + u] = p
                    l = l + fold(p, jnp.sum)
                    dl = dl + fold(p * wbuf[ki * subs + u], jnp.sum)
                return l, dl

            none = jnp.zeros((8, BLK), f32)
            l, dl = lax.fori_loop(0, supers, middle, (none, none))
            inv_l = 1.0 / jnp.sum(l, axis=0, keepdims=True)
            delta = jnp.sum(dl, axis=0, keepdims=True) * inv_l
            both = qg[qi]

            def last(ki, dq):
                for u in range(subs):
                    kat = pl.multiple_of(ki * KBLK + u * BLK, BLK)
                    att = sbuf[ki * subs + u] * inv_l
                    ds = (att * (wbuf[ki * subs + u] - delta)).astype(bf16)
                    pair = jnp.concatenate([ds, att.astype(bf16)], axis=1)
                    dkv[pl.ds(kat, BLK), :] += dot(pair, both)
                    dq = dq + dot(kt[ki * subs + u], ds)
                return dq

            dq = lax.fori_loop(0, supers, last, jnp.zeros((hd, BLK), f32))
            dq = jnp.concatenate([dq * inv_root, jnp.zeros((hd, BLK), f32)], axis=0)
            dqp[pl.ds(at, BLK), :] = dq.T
            return c

        lax.fori_loop(0, blocks, per_queries, 0)

        def unpack(r, off):
            off = pl.multiple_of(off, 16)
            count = cnt_ref[r, 0, 0]
            live = lax.broadcasted_iota(jnp.int32, (t, width), 0) < count
            both = jnp.where(live, dkv[pl.ds(off, t), :], 0.0)
            dq = jnp.where(live, dqp[pl.ds(off, t), :], 0.0)
            out_ref[r, 0:t, :] = both.astype(bf16)
            pair = jnp.concatenate([dq[0 : t // 2, 0:hd], dq[t // 2 :, 0:hd]], axis=1)
            out_ref[r, t:, :] = pair.astype(bf16)
            return off + (count + 15) // 16 * 16

        lax.fori_loop(0, n_reg, unpack, 0, unroll=4)


def collect_kernel(
    n_reg, n_tm, part_ref, ck_ref, wq_ref, wk_ref, wv_ref,
    out_ref,
    got, wbuf, xs, ext, wsem, esem, ssem, rsem, lsem,
):
    me = lax.axis_index("region")
    mt = lax.axis_index("tm")
    t, d = out_ref.shape[1], out_ref.shape[2]
    hd = d // H
    loads = [
        pltpu.make_async_copy(ref, wbuf.at[i], wsem.at[i])
        for i, ref in enumerate((wq_ref, wk_ref, wv_ref))
    ]
    for load in loads:
        load.start()
    barrier = pltpu.get_barrier_semaphore()
    head, is_head = head_of(me, n_reg)
    for i in range(H):
        target = owner(lax.rem(me + i, H), n_reg)

        @pl.when(target != me)
        def _():
            greet(barrier, region=target)

    @pl.when(mt < n_tm - 1)
    def _():
        greet(barrier, tm=jnp.minimum(mt + 1, n_tm - 1))

    peers = jnp.where(is_head, n_reg - 1, 0) + jnp.minimum(mt, 1)

    @pl.when(peers > 0)
    def _():
        pl.semaphore_wait(barrier, peers)

    head = jnp.minimum(head, H - 1)

    def away(k):
        r = lax.rem(me + k, n_reg)
        return pltpu.make_async_remote_copy(
            src_ref=part_ref.at[r],
            dst_ref=got.at[head],
            send_sem=ssem.at[k],
            recv_sem=rsem.at[head],
            device_id={"region": r},
            device_id_type=MESH,
        )

    here = pltpu.make_async_copy(part_ref.at[me], got.at[head], lsem)

    @pl.when(is_head)
    def _():
        for k in range(1, n_reg):
            away(k).start()
        here.start()
        here.wait()

    for h in range(H):

        @pl.when(owner(h, n_reg) != me)
        def _():
            pltpu.make_async_copy(part_ref.at[0], got.at[h], rsem.at[h]).wait()

    for h in range(H):
        cols = slice(h * hd, (h + 1) * hd)
        xs[0, 0 : t // 2, cols] = got[h, t:, 0:hd]
        xs[0, t // 2 :, cols] = got[h, t:, hd:]
        xs[1, :, cols] = got[h, 0:t, 0:hd]
        xs[2, :, cols] = got[h, 0:t, hd:]
    for load in loads:
        load.wait()
    side = dot_t(xs[1], wbuf[1]) + dot_t(xs[2], wbuf[2])
    ext[0:t, :] = dot_t(xs[0], wbuf[0]) + side

    to_prev = pltpu.make_async_remote_copy(
        src_ref=ext.at[pl.ds(0, 8)],
        dst_ref=ext.at[pl.ds(t, 8)],
        send_sem=esem.at[0],
        recv_sem=esem.at[1],
        device_id={"tm": jnp.maximum(mt - 1, 0)},
        device_id_type=MESH,
    )

    @pl.when(mt > 0)
    def _():
        to_prev.start()

    @pl.when(is_head)
    def _():
        for k in range(1, n_reg):
            away(k).wait_send()

    @pl.when(mt == n_tm - 1)
    def _():
        ext[t : t + 8, :] = jnp.zeros((8, d), f32)

    @pl.when(mt < n_tm - 1)
    def _():
        to_prev.wait_recv()

    total = ck_ref[0:1, :] * ext[0:t, :]
    for j in range(1, KW):
        total = total + ck_ref[j : j + 1, :] * ext[j : j + t, :]
    out_ref[0] = total.astype(bf16)

    @pl.when(mt > 0)
    def _():
        to_prev.wait_send()


def shards(n_reg, n_tm, latents, output_grad, conv_kernel, w_query, w_key, w_value, w_out, live_counts):
    _, t, d = latents.shape
    hd = d // H
    dma = pltpu.SemaphoreType.DMA
    n = n_reg * t
    blocks = -(-n // KBLK) * (KBLK // BLK)
    chunks, counts = pl.pallas_call(
        functools.partial(spread_kernel, n_reg, n_tm),
        out_shape=(
            jax.ShapeDtypeStruct((n_reg, t, 4 * hd), bf16),
            jax.ShapeDtypeStruct((n_reg, 1, 128), jnp.int32),
        ),
        in_specs=[VM, VM, VM, SM, ANY, ANY, ANY, ANY],
        out_specs=(ANY, ANY),
        scratch_shapes=[
            pltpu.VMEM((4, d, d), bf16),
            pltpu.VMEM((t + 8, d), f32),
            pltpu.VMEM((16, d), bf16),
            pltpu.VMEM((H, t, 4 * hd), bf16),
            pltpu.VMEM((1, 128), jnp.int32),
            dma((4,)),
            dma((2,)),
            dma((3, H)),
            dma((3, n_reg)),
            dma((2,)),
        ],
        compiler_params=pltpu.CompilerParams(collective_id=0, has_side_effects=True),
        name="spread",
    )(latents, output_grad, conv_kernel, live_counts, w_query, w_key, w_value, w_out)
    part = pl.pallas_call(
        functools.partial(attend_kernel, n_reg, hd),
        out_shape=jax.ShapeDtypeStruct((n_reg, t + t // 2, 2 * hd), bf16),
        in_specs=[VM, SM],
        out_specs=VM,
        scratch_shapes=[
            pltpu.VMEM((n + KBLK, 2 * hd), bf16),
            pltpu.VMEM((n + KBLK, 2 * hd), bf16),
            pltpu.VMEM((n + KBLK, 2 * hd), bf16),
            pltpu.VMEM((blocks, hd, BLK), bf16),
            pltpu.VMEM((blocks, 2 * hd, BLK), bf16),
            pltpu.VMEM((blocks, 2 * hd, BLK), bf16),
            pltpu.VMEM((blocks, 2 * BLK, 2 * hd), bf16),
            pltpu.VMEM((blocks, BLK, BLK), f32),
            pltpu.VMEM((blocks, BLK, BLK), f32),
            pltpu.VMEM((n + KBLK, 2 * hd), f32),
            pltpu.VMEM((n + KBLK, 2 * hd), f32),
        ],
        name="attend",
    )(chunks, counts)
    return pl.pallas_call(
        functools.partial(collect_kernel, n_reg, n_tm),
        out_shape=jax.ShapeDtypeStruct((1, t, d), bf16),
        in_specs=[ANY, VM, ANY, ANY, ANY],
        out_specs=VM,
        scratch_shapes=[
            pltpu.VMEM((H, t + t // 2, 2 * hd), bf16),
            pltpu.VMEM((3, d, d), bf16),
            pltpu.VMEM((3, t, d), bf16),
            pltpu.VMEM((t + 8, d), f32),
            dma((3,)),
            dma((2,)),
            dma((n_reg,)),
            dma((H,)),
            dma,
        ],
        compiler_params=pltpu.CompilerParams(collective_id=1, has_side_effects=True),
        name="collect",
    )(part, conv_kernel, w_query, w_key, w_value)


def solution(mesh):
    shard = P("region", "tm", None)
    in_specs = (shard, shard, P(), P(), P(), P(), P(), P("region", "tm"))
    body = functools.partial(shards, mesh.shape["region"], mesh.shape["tm"])
    return jax.shard_map(body, mesh=mesh, in_specs=in_specs, out_specs=shard, check_vma=False)
```

profile of v0, /device:TPU:14, one launch (start us, length us, event | category | flops | bytes accessed | tf_op | source)
XLA Modules:
  0.0 61.7 jit_solution(16106021361280017672)
XLA Ops:
  0.7 22.4 %spread.1 = (bf16[16,128,256]{2,1,0:T(8,128)(2,1)}, s32[16,1,128]{2,1,0:T(1,128)}) custom-call(bf16[1,128,768]{2,1,0:T(8,128)(2,1)} %lat_ref.1, bf16[1,128,768]{2,1,0:T(8,128)(2,1)} %og_ref.1, f32[4,768]{1,0:T(4,128)} %ck_ref.3, s32[1,1]{1,0:T(1,128)S(6)} %copy.10.cnt_ref, bf16[768,768]{1,0:T(8,128)(2,1)} %wq_ref.3, bf16[768,768]{1,0:T(8,128)(2,1)} %wk_ref.3, ...), custom_call_target="tpu_custom_call" | custom-call | tf_op jit(solution)/shard_map/spread/pallas_call | solution.py:421
  23.1 2.2 %attend.1.part_ref = bf16[16,192,128]{2,1,0:T(8,128)(2,1)} custom-call(bf16[16,128,256]{2,1,0:T(8,128)(2,1)} %get-tuple-element.7.chunk_ref, s32[16,1,128]{2,1,0:T(1,128)} %get-tuple-element.8.cnt_ref), custom_call_target="tpu_custom_call" | custom-call | tf_op jit(solution)/shard_map/attend/pallas_call | solution.py:444
  25.3 34.8 %collect.1 = bf16[1,128,768]{2,1,0:T(8,128)(2,1)} custom-call(bf16[16,192,128]{2,1,0:T(8,128)(2,1)} %attend.1.part_ref, f32[4,768]{1,0:T(4,128)} %ck_ref.3, bf16[768,768]{1,0:T(8,128)(2,1)} %wq_ref.3, bf16[768,768]{1,0:T(8,128)(2,1)} %wk_ref.3, bf16[768,768]{1,0:T(8,128)(2,1)} %wv_ref.3), custom_call_target="tpu_custom_call" | custom-call | tf_op jit(solution)/shard_map/collect/pallas_call | solution.py:464
  60.1 1.6 %copy.11 = bf16[1,128,768]{2,1,0:T(8,128)(2,1)} copy(bf16[1,128,768]{2,1,0:T(8,128)(2,1)} %collect.1) | data formatting | bytes 393216
where the time goes:
time: 61.3 us; the launch traced here: 61.7 us
  Pallas kernels  59.5 us (97%)
  local copies, waits for them, and re-layouts  1.62 us (3%)
  between operations  0.67 us (1%)
    pallas_call x1, Pallas kernels, shards(): pl.pallas_call(functools.partial(collect_kernel, n_reg, n_tm), out_shape=...  34.8 us
    pallas_call x1, Pallas kernels, shards(): pl.pallas_call(functools.partial(spread_kernel, n_reg, n_tm), out_shape=(...  22.4 us
    pallas_call x1, Pallas kernels, shards(): pl.pallas_call(functools.partial(attend_kernel, n_reg, hd), out_shape=jax...  2.19 us
    unnamed x1, local copies, waits for them, and re-layouts  1.62 us

commit v1 on v0

v1 whole, which is shorter than its diff:
```python
import functools
import math

import jax
import jax.numpy as jnp
from jax import lax
from jax.experimental import pallas as pl
from jax.experimental.pallas import tpu as pltpu
from jax.sharding import PartitionSpec as P

H = 12
KW = 4
BLK = 256
PAGE = 16
CAPS = (1024, 1280)
NEG = -1e30
bf16 = jnp.bfloat16
f32 = jnp.float32
i32 = jnp.int32
VM = pl.BlockSpec(memory_space=pltpu.VMEM)
SM = pl.BlockSpec(memory_space=pltpu.SMEM)
ANY = pl.BlockSpec(memory_space=pl.ANY)
MESH = pl.DeviceIdType.MESH


def dot(a, b):
    return jnp.dot(a, b, preferred_element_type=f32)


def dot_t(a, b):
    return lax.dot_general(a, b, (((1,), (1,)), ((), ())), preferred_element_type=f32)


def owner(h, n_reg):
    return (h * n_reg) // H


def head_of(me, n_reg):
    h = (me * H + n_reg - 1) // n_reg
    return jnp.minimum(h, H - 1), jnp.logical_and(h < H, owner(h, n_reg) == me)


def peer(me, step, n):
    if n & (n - 1):
        return lax.rem(me + step, n)
    out = me
    for b in range(n.bit_length() - 1):
        if step >> b & 1:
            w = 1 << b
            out = out + w * (1 - 2 * ((me // w) % 2))
    return out


def caps_of(n):
    return [c for c in CAPS if c < n] + [-(-n // 1024) * 1024]


def spread_kernel(
    n_reg, n_tm, caps, lat_ref, og_ref, ck_ref, cnt_ref, wq_ref, wk_ref, wv_ref, wo_ref,
    out_ref, table_ref, pick_ref,
    wbuf, lat, og, ext, edge, send, csend, cbuf, wsem, esem, ssem, rsem, tsem, lsem,
):
    me = lax.axis_index("region")
    mt = lax.axis_index("tm")
    t, d = lat_ref.shape[1], lat_ref.shape[2]
    hd = d // H
    barrier = pltpu.get_barrier_semaphore()
    others = [
        (k, c) for k in reversed(range(n_reg)) for c in range(n_tm) if (k, c) != (0, 0)
    ]

    def place(k, c):
        return {"region": peer(me, k, n_reg), "tm": lax.rem(mt + c, n_tm)}

    for k, c in others:
        pl.semaphore_signal(barrier, inc=1, device_id=place(k, c), device_id_type=MESH)
    loads = [
        pltpu.make_async_copy(ref, dst, wsem.at[i])
        for i, (ref, dst) in enumerate(
            (
                (lat_ref.at[0], lat),
                (og_ref.at[0], og),
                (wo_ref, wbuf.at[0]),
                (wv_ref, wbuf.at[1]),
                (wq_ref, wbuf.at[2]),
                (wk_ref, wbuf.at[3]),
            )
        )
    ]
    for load in loads:
        load.start()
    head, is_head = head_of(me, n_reg)

    count = cnt_ref[0, 0]
    csend[...] = jnp.zeros(csend.shape, i32) + count
    cbuf[mt, me] = jnp.zeros(csend.shape, i32) + count

    def hide(rows):
        hidden = ck_ref[0:1, :] * ext[8 : 8 + rows, :]
        for j in range(1, KW):
            hidden = hidden + ck_ref[j : j + 1, :] * ext[8 - j : 8 - j + rows, :]
        return hidden.astype(bf16)

    def put(x, rows, half, first):
        for h in range(H):
            part = x[:, h * hd : (h + 1) * hd].reshape(rows // PAGE, PAGE, hd)
            send[h, half, 0 : rows // PAGE, :, first : first + hd] = part

    loads[0].wait()
    ext[0:8, :] = jnp.zeros((8, d), f32)
    ext[8 : 8 + t, :] = lat[...].astype(f32)
    hidden = hide(t)
    loads[1].wait()
    loads[2].wait()
    live = lax.broadcasted_iota(i32, (t, 1), 0) < count
    g = jnp.where(live, dot_t(og[...], wbuf[0]), 0.0).astype(bf16)
    put(g, t, 1, hd)
    loads[3].wait()
    put(dot(hidden, wbuf[1]).astype(bf16), t, 1, 0)

    pl.semaphore_wait(barrier, len(others))
    to_next = pltpu.make_async_remote_copy(
        src_ref=lat.at[pl.ds(t - 16, 16)],
        dst_ref=edge,
        send_sem=esem.at[0],
        recv_sem=esem.at[1],
        device_id={"tm": jnp.minimum(mt + 1, n_tm - 1)},
        device_id_type=MESH,
    )

    @pl.when(mt < n_tm - 1)
    def _():
        to_next.start()

    parts = (
        (1, pl.ds(1, t // PAGE - 1)),
        (0, pl.ds(1, t // PAGE - 1)),
        (slice(None), pl.ds(0, 1)),
    )

    def away(k, i):
        target = peer(me, k, n_reg)
        half, rows = parts[i]
        return pltpu.make_async_remote_copy(
            src_ref=send.at[head_of(target, n_reg)[0], half, rows],
            dst_ref=out_ref.at[half, me, rows],
            send_sem=ssem.at[i, k],
            recv_sem=rsem.at[i, me],
            device_id={"region": target},
            device_id_type=MESH,
        )

    def each(act):
        for k in reversed(range(1, n_reg)):

            @pl.when(head_of(peer(me, k, n_reg), n_reg)[1])
            def _():
                act(k)

    def tell(j):
        return pltpu.make_async_remote_copy(
            src_ref=csend,
            dst_ref=cbuf.at[mt, me],
            send_sem=tsem.at[0, j],
            recv_sem=tsem.at[1, mt * n_reg + me],
            device_id=place(*others[j]),
            device_id_type=MESH,
        )

    each(lambda k: away(k, 0).start())
    for j in range(len(others)):
        tell(j).start()
    loads[4].wait()
    put(dot(hidden, wbuf[2]).astype(bf16), t, 0, 0)
    loads[5].wait()
    put(dot(hidden, wbuf[3]).astype(bf16), t, 0, hd)
    each(lambda k: away(k, 1).start())

    @pl.when(mt > 0)
    def _():
        to_next.wait_recv()
        ext[0:8, :] = edge[8:16, :].astype(f32)
        top = hide(16)
        put(dot(top, wbuf[1]).astype(bf16), 16, 1, 0)
        put(dot(top, wbuf[2]).astype(bf16), 16, 0, 0)
        put(dot(top, wbuf[3]).astype(bf16), 16, 0, hd)

    each(lambda k: away(k, 2).start())
    here = pltpu.make_async_copy(send.at[head], out_ref.at[:, me], lsem.at[0])

    @pl.when(is_head)
    def _():
        here.start()

    for j in range(len(others)):
        k, c = others[j]
        where = place(k, c)
        slot = where["tm"] * n_reg + where["region"]
        pltpu.make_async_copy(csend, cbuf.at[where["tm"], where["region"]], tsem.at[1, slot]).wait()
    pages = t // PAGE
    zero = jnp.zeros(csend.shape, i32)
    slot = lax.broadcasted_iota(i32, csend.shape, 1)

    def used(c, r):
        return (cbuf[c, r] + (PAGE - 1)) // PAGE

    most = zero
    for c in range(n_tm):
        total = zero
        for r in range(n_reg):
            total = total + used(c, r)
        most = jnp.maximum(most, total)
    pick = zero
    for cap in caps[:-1]:
        pick = pick + jnp.where(most * PAGE > cap, 1, 0)
    pick_ref[0, 0] = jnp.max(pick.astype(f32)).astype(i32)
    end, source, rows_left, begin = zero, zero, zero, zero
    for r in range(n_reg):
        n = used(mt, r)
        mine = jnp.logical_and(slot >= end, slot < end + n)
        source = jnp.where(mine, slot - end + r * pages, source)
        rows_left = jnp.where(mine, cbuf[mt, r] - (slot - end) * PAGE, rows_left)
        begin = jnp.where(slot == r, end, begin)
        end = end + n
    counts = zero
    for r in range(n_reg):
        counts = jnp.where(slot == r, cbuf[mt, r], counts)
    for i, row in enumerate((source, rows_left, begin, counts)):
        table_ref[i : i + 1, :] = row

    def done(k):
        for i in range(3):
            away(k, i).wait_send()

    each(done)
    for j in range(len(others)):
        tell(j).wait_send()

    @pl.when(mt < n_tm - 1)
    def _():
        to_next.wait_send()

    @pl.when(is_head)
    def _():
        here.wait()
        for k in range(1, n_reg):
            s = peer(me, k, n_reg)
            for i, (half, rows) in enumerate(parts):
                there = out_ref.at[half, s, rows]
                pltpu.make_async_copy(send.at[0, half, rows], there, rsem.at[i, s]).wait()


def work_kernel(
    n_reg, n_tm, cap, chunk_ref, tbl_ref, ck_ref, wq_ref, wk_ref, wv_ref,
    out_ref,
    chunk, qk, ka, vg, kt, qt, gt, qg, sbuf, wbuf, dkv, dqp, part,
    got, wts, xs, ext, wsem, esem, ssem, rsem, lsem,
):
    me = lax.axis_index("region")
    mt = lax.axis_index("tm")
    t, d = out_ref.shape[1], out_ref.shape[2]
    hd = d // H
    width = 2 * hd
    inv_root = 1.0 / math.sqrt(hd)
    blocks = cap // BLK
    subs = blocks if blocks <= 5 else 4
    supers = blocks // subs
    step = BLK // PAGE
    barrier = pltpu.get_barrier_semaphore()
    head, is_head = head_of(me, n_reg)

    def each(act):
        for k in reversed(range(1, n_reg)):
            r = peer(me, k, n_reg)

            @pl.when(head_of(r, n_reg)[1])
            def _():
                act(r)

    each(
        lambda r: pl.semaphore_signal(
            barrier, inc=1, device_id={"region": r}, device_id_type=MESH
        )
    )

    @pl.when(mt < n_tm - 1)
    def _():
        up = {"tm": jnp.minimum(mt + 1, n_tm - 1)}
        pl.semaphore_signal(barrier, inc=1, device_id=up, device_id_type=MESH)

    fetch = pltpu.make_async_copy(chunk_ref, chunk, lsem.at[1])

    @pl.when(is_head)
    def _():
        fetch.start()

    loads = [
        pltpu.make_async_copy(ref, wts.at[i], wsem.at[i])
        for i, ref in enumerate((wq_ref, wk_ref, wv_ref))
    ]
    for load in loads:
        load.start()
    peers = jnp.where(is_head, n_reg - 1, 0) + jnp.minimum(mt, 1)

    def lane(rows):
        return lax.broadcasted_iota(i32, (rows, width), 1)

    def away(r, k):
        return pltpu.make_async_remote_copy(
            src_ref=part.at[r],
            dst_ref=got.at[head],
            send_sem=ssem.at[k],
            recv_sem=rsem.at[head],
            device_id={"region": r},
            device_id_type=MESH,
        )

    here = pltpu.make_async_copy(part.at[me], got.at[head], lsem.at[0])

    @pl.when(is_head)
    def _():
        fetch.wait()

        def pack(p, c):
            source = tbl_ref[0, p]
            rows = tbl_ref[1, p]
            a = chunk[0, source]
            b = chunk[1, source]
            dead = lax.broadcasted_iota(i32, (PAGE, width), 0) >= rows
            bias = jnp.where(jnp.logical_and(lane(PAGE) == 0, dead), NEG, 0.0)
            to = pl.ds(pl.multiple_of(p * PAGE, PAGE), PAGE)
            qk[to, :] = a
            ka[to, :] = jnp.where(lane(PAGE) < hd, bias, a.astype(f32)).astype(bf16)
            vg[to, :] = jnp.where(dead, 0.0, b.astype(f32)).astype(bf16)
            return c

        lax.fori_loop(0, cap // PAGE, pack, 0, unroll=4)

        def ready(i, c):
            at = pl.multiple_of(i * BLK, BLK)
            a = qk[pl.ds(at, BLK), :]
            b = vg[pl.ds(at, BLK), :]
            a_t = a.T
            scaled = (a_t[0:hd, :].astype(f32) * inv_root).astype(bf16)
            one = jnp.where(lax.broadcasted_iota(i32, (hd, BLK), 0) == 0, 1.0, 0.0)
            qt[i] = jnp.concatenate([one.astype(bf16), scaled], axis=0)
            kt[i] = a_t[hd:, :]
            gt[i] = jnp.concatenate([b.T[hd:, :], jnp.zeros((hd, BLK), bf16)], axis=0)
            low = lane(BLK) < hd
            qg[i, 0:BLK, :] = jnp.where(low, a.astype(f32) * inv_root, 0.0).astype(bf16)
            qg[i, BLK:, :] = jnp.where(low, 0.0, b.astype(f32)).astype(bf16)
            dkv[pl.ds(i * step, step)] = jnp.zeros((step, PAGE, width), f32)
            return c

        lax.fori_loop(0, blocks, ready, 0)

        def fold(x, op):
            return op(x.reshape(BLK // 8, 8, BLK), axis=0)

        def per_queries(qi, c):
            qat, gat = qt[qi], gt[qi]

            def first(ki, m):
                for u in range(subs):
                    kat = pl.multiple_of((ki * subs + u) * BLK, BLK)
                    s = dot(ka[pl.ds(kat, BLK), :], qat)
                    wbuf[ki * subs + u] = dot(vg[pl.ds(kat, BLK), :], gat)
                    sbuf[ki * subs + u] = s
                    m = jnp.maximum(m, fold(s, jnp.max))
                return m

            m = lax.fori_loop(0, supers, first, jnp.full((8, BLK), NEG, f32))
            m = jnp.max(m, axis=0, keepdims=True)

            def middle(ki, carry):
                l, dl = carry
                for u in range(subs):
                    p = jnp.exp(sbuf[ki * subs + u] - m)
                    sbuf[ki * subs + u] = p
                    l = l + fold(p, jnp.sum)
                    dl = dl + fold(p * wbuf[ki * subs + u], jnp.sum)
                return l, dl

            none = jnp.zeros((8, BLK), f32)
            l, dl = lax.fori_loop(0, supers, middle, (none, none))
            inv_l = 1.0 / jnp.sum(l, axis=0, keepdims=True)
            delta = jnp.sum(dl, axis=0, keepdims=True) * inv_l
            both = qg[qi]

            def last(ki, dq):
                for u in range(subs):
                    att = sbuf[ki * subs + u] * inv_l
                    ds = (att * (wbuf[ki * subs + u] - delta)).astype(bf16)
                    pair = jnp.concatenate([ds, att.astype(bf16)], axis=1)
                    to = pl.ds((ki * subs + u) * step, step)
                    dkv[to] += dot(pair, both).reshape(step, PAGE, width)
                    dq = dq + dot(kt[ki * subs + u], ds)
                return dq

            dq = lax.fori_loop(0, supers, last, jnp.zeros((hd, BLK), f32))
            dq = jnp.concatenate([dq * inv_root, jnp.zeros((hd, BLK), f32)], axis=0)
            dqp[pl.ds(qi * step, step)] = dq.T.reshape(step, PAGE, width)
            return c

        lax.fori_loop(0, blocks, per_queries, 0)

    @pl.when(peers > 0)
    def _():
        pl.semaphore_wait(barrier, peers)

    @pl.when(is_head)
    def _():
        for k in reversed(range(n_reg)):
            r = peer(me, k, n_reg)
            begin = tbl_ref[2, r]
            live = lax.broadcasted_iota(i32, (t, width), 0) < tbl_ref[3, r]

            def rows_of(ref):
                pages = [ref[begin + j] for j in range(t // PAGE)]
                return jnp.where(live, jnp.concatenate(pages, axis=0), 0.0)

            both, dq = rows_of(dkv), rows_of(dqp)
            part[r, 0:t, :] = both.astype(bf16)
            pair = jnp.concatenate([dq[0 : t // 2, 0:hd], dq[t // 2 :, 0:hd]], axis=1)
            part[r, t:, :] = pair.astype(bf16)
            if k:
                away(r, k).start()
            else:
                here.start()
        here.wait()

    for h in range(H):

        @pl.when(owner(h, n_reg) != me)
        def _():
            pltpu.make_async_copy(part.at[0], got.at[h], rsem.at[h]).wait()

    for h in range(H):
        cols = slice(h * hd, (h + 1) * hd)
        xs[0, 0 : t // 2, cols] = got[h, t:, 0:hd]
        xs[0, t // 2 :, cols] = got[h, t:, hd:]
        xs[1, :, cols] = got[h, 0:t, 0:hd]
        xs[2, :, cols] = got[h, 0:t, hd:]
    for load in loads:
        load.wait()
    side = dot_t(xs[1], wts[1]) + dot_t(xs[2], wts[2])
    ext[0:t, :] = dot_t(xs[0], wts[0]) + side

    to_prev = pltpu.make_async_remote_copy(
        src_ref=ext.at[pl.ds(0, 8)],
        dst_ref=ext.at[pl.ds(t, 8)],
        send_sem=esem.at[0],
        recv_sem=esem.at[1],
        device_id={"tm": jnp.maximum(mt - 1, 0)},
        device_id_type=MESH,
    )

    @pl.when(mt > 0)
    def _():
        to_prev.start()

    @pl.when(is_head)
    def _():
        for k in range(1, n_reg):
            away(peer(me, k, n_reg), k).wait_send()

    @pl.when(mt == n_tm - 1)
    def _():
        ext[t : t + 8, :] = jnp.zeros((8, d), f32)

    @pl.when(mt < n_tm - 1)
    def _():
        to_prev.wait_recv()

    total = ck_ref[0:1, :] * ext[0:t, :]
    for j in range(1, KW):
        total = total + ck_ref[j : j + 1, :] * ext[j : j + t, :]
    out_ref[0] = total.astype(bf16)

    @pl.when(mt > 0)
    def _():
        to_prev.wait_send()


def shards(n_reg, n_tm, latents, output_grad, conv_kernel, w_query, w_key, w_value, w_out, live_counts):
    _, t, d = latents.shape
    hd = d // H
    dma = pltpu.SemaphoreType.DMA
    caps = caps_of(n_reg * t)
    lanes = max(128, n_reg * t // PAGE)
    chunks, table, pick = pl.pallas_call(
        functools.partial(spread_kernel, n_reg, n_tm, caps),
        out_shape=(
            jax.ShapeDtypeStruct((2, n_reg, t // PAGE, PAGE, 2 * hd), bf16),
            jax.ShapeDtypeStruct((4, lanes), i32),
            jax.ShapeDtypeStruct((1, 1), i32),
        ),
        in_specs=[ANY, ANY, VM, SM, ANY, ANY, ANY, ANY],
        out_specs=(ANY, VM, SM),
        scratch_shapes=[
            pltpu.VMEM((4, d, d), bf16),
            pltpu.VMEM((t, d), bf16),
            pltpu.VMEM((t, d), bf16),
            pltpu.VMEM((t + 8, d), f32),
            pltpu.VMEM((16, d), bf16),
            pltpu.VMEM((H, 2, t // PAGE, PAGE, 2 * hd), bf16),
            pltpu.VMEM((1, lanes), i32),
            pltpu.VMEM((n_tm, n_reg, 1, lanes), i32),
            dma((6,)),
            dma((2,)),
            dma((3, n_reg)),
            dma((3, n_reg)),
            dma((2, n_reg * n_tm)),
            dma((1,)),
        ],
        compiler_params=pltpu.CompilerParams(collective_id=0, has_side_effects=True),
        name="spread",
    )(latents, output_grad, conv_kernel, live_counts, w_query, w_key, w_value, w_out)

    def work(i, cap):
        blocks = cap // BLK
        return pl.pallas_call(
            functools.partial(work_kernel, n_reg, n_tm, cap),
            out_shape=jax.ShapeDtypeStruct((1, t, d), bf16),
            in_specs=[ANY, SM, VM, ANY, ANY, ANY],
            out_specs=VM,
            scratch_shapes=[
                pltpu.VMEM((2, n_reg * t // PAGE, PAGE, 2 * hd), bf16),
                pltpu.VMEM((cap, 2 * hd), bf16),
                pltpu.VMEM((cap, 2 * hd), bf16),
                pltpu.VMEM((cap, 2 * hd), bf16),
                pltpu.VMEM((blocks, hd, BLK), bf16),
                pltpu.VMEM((blocks, 2 * hd, BLK), bf16),
                pltpu.VMEM((blocks, 2 * hd, BLK), bf16),
                pltpu.VMEM((blocks, 2 * BLK, 2 * hd), bf16),
                pltpu.VMEM((blocks, BLK, BLK), f32),
                pltpu.VMEM((blocks, BLK, BLK), f32),
                pltpu.VMEM(((cap + t) // PAGE, PAGE, 2 * hd), f32),
                pltpu.VMEM(((cap + t) // PAGE, PAGE, 2 * hd), f32),
                pltpu.VMEM((n_reg, t + t // 2, 2 * hd), bf16),
                pltpu.VMEM((H, t + t // 2, 2 * hd), bf16),
                pltpu.VMEM((3, d, d), bf16),
                pltpu.VMEM((3, t, d), bf16),
                pltpu.VMEM((t + 8, d), f32),
                dma((3,)),
                dma((2,)),
                dma((n_reg,)),
                dma((H,)),
                dma((2,)),
            ],
            compiler_params=pltpu.CompilerParams(collective_id=i + 1, has_side_effects=True),
            name=f"work{cap}",
        )

    return lax.switch(
        pick[0, 0],
        [work(i, cap) for i, cap in enumerate(caps)],
        chunks.reshape(2, n_reg * t // PAGE, PAGE, 2 * hd), table, conv_kernel, w_query, w_key, w_value,
    )


def solution(mesh):
    shard = P("region", "tm", None)
    in_specs = (shard, shard, P(), P(), P(), P(), P(), P("region", "tm"))
    body = functools.partial(shards, mesh.shape["region"], mesh.shape["tm"])
    return jax.shard_map(body, mesh=mesh, in_specs=in_specs, out_specs=shard, check_vma=False)
```

time: 61.3 us -> 62.3 us (1.016)
  the two profiles are of different devices: /device:TPU:14 before, /device:TPU:0 now
where the time goes in v1:
time: 62.3 us; the launch traced here: 62.1 us
  Pallas kernels  58.9 us (95%)
  local copies, waits for them, and re-layouts  1.63 us (3%)
  between operations  1.35 us (2%)
    pallas_call x1, Pallas kernels, shards(): lax.switch(pick[0, 0], [work(i, cap) for i, cap in enumerate(caps)], chun...  29.4 us
    pallas_call x1, Pallas kernels, shards(): pl.pallas_call(functools.partial(spread_kernel, n_reg, n_tm, caps), out_s...  29.4 us
    unnamed x9, local copies, waits for them, and re-layouts  1.63 us

profile of v1, /device:TPU:0, one launch (start us, length us, event | category | flops | bytes accessed | tf_op | source)
XLA Modules:
  0.0 62.1 jit_solution(3239988083569370053)
XLA Ops:
  0.7 0.0 copy-start
  0.7 0.0 copy-start.1
  0.7 0.0 copy-start.2
  0.7 0.0 copy-start.3
  0.7 29.4 %spread.1 = (bf16[2,16,8,16,128]{4,3,2,1,0:T(8,128)(2,1)}, s32[4,128]{1,0:T(4,128)S(1)}, s32[1,1]{1,0:T(1,128)}) custom-call(bf16[1,128,768]{2,1,0:T(8,128)(2,1)} %lat_ref.1, bf16[1,128,768]{2,1,0:T(8,128)(2,1)} %og_ref.1, f32[4,768]{1,0:T(4,128)} %ck_ref.1, s32[1,1]{1,0:T(1,128)S(6)} %copy.16.cnt_ref, bf16[768,768]{1,0:T(8,128)(2,1)} %wq_ref.1, ...), custom_call_target="tpu_custom_call" | custom-call | tf_op jit(solution)/shard_map/spread/pallas_call | solution.py:491
  30.7 0.0 copy-done
  30.8 0.0 copy-done.1
  30.8 0.0 copy-done.2
  30.8 0.0 copy-done.3
  30.8 29.7 %conditional.1 = (bf16[1,128,768]{2,1,0:T(8,128)(2,1)}) conditional(s32[]{:T(128)} %bitcast, (bf16[2,128,16,128]{3,2,1,0:T(8,128)(2,1)}, s32[4,128]{1,0:T(4,128)S(1)}, f32[4,768]{1,0:T(4,128)S(1)}, bf16[768,768]{1,0:T(8,128)(2,1)S(1)}, bf16[768,768]{1,0:T(8,128)(2,1)S(1)}, /*index=5*/bf16[768,768]{1,0:T(8,128)(2,1)S(1)}) %tuple.33, ...), branch_computations={%region_0.0_spmd, %region_1.0_spmd, %region_2.0_spmd} | conditional | bytes 8 | solution.py:555
  30.8 29.4 %work1024.1 = bf16[1,128,768]{2,1,0:T(8,128)(2,1)} custom-call(bf16[2,128,16,128]{3,2,1,0:T(8,128)(2,1)} %get-tuple-element.44.chunk_ref, s32[4,128]{1,0:T(4,128)S(1)} %get-tuple-element.46.tbl_ref, f32[4,768]{1,0:T(4,128)S(1)} %get-tuple-element.47.ck_ref, bf16[768,768]{1,0:T(8,128)(2,1)S(1)} %get-tuple-element.48.wq_ref, ...), custom_call_target="tpu_custom_call" | custom-call | tf_op jit(solution)/shard_map/cond/branch_0_fun/work1024/pallas_call | solution.py:555
  60.5 1.6 %copy.17 = bf16[1,128,768]{2,1,0:T(8,128)(2,1)} copy(bf16[1,128,768]{2,1,0:T(8,128)(2,1)} %get-tuple-element.69) | data formatting | bytes 393216
Async XLA Ops:
  0.7 30.1 %copy-start = (bf16[768,768]{1,0:T(8,128)(2,1)S(1)}, bf16[768,768]{1,0:T(8,128)(2,1)}, u32[]{:S(2)}) copy-start(bf16[768,768]{1,0:T(8,128)(2,1)} %wq_ref.1) | copy-start | bytes 3538948
  0.7 30.1 %copy-start.1 = (bf16[768,768]{1,0:T(8,128)(2,1)S(1)}, bf16[768,768]{1,0:T(8,128)(2,1)}, u32[]{:S(2)}) copy-start(bf16[768,768]{1,0:T(8,128)(2,1)} %wk_ref.1) | copy-start | bytes 3538948
  0.7 30.1 %copy-start.2 = (bf16[768,768]{1,0:T(8,128)(2,1)S(1)}, bf16[768,768]{1,0:T(8,128)(2,1)}, u32[]{:S(2)}) copy-start(bf16[768,768]{1,0:T(8,128)(2,1)} %wv_ref.1) | copy-start | bytes 3538948
  0.7 30.1 %copy-start.3 = (f32[4,768]{1,0:T(4,128)S(1)}, f32[4,768]{1,0:T(4,128)}, u32[]{:S(2)}) copy-start(f32[4,768]{1,0:T(4,128)} %ck_ref.1) | copy-start | bytes 36868

commit v2 on v1

--- a/solution.py
+++ b/solution.py
@@ -31,24 +31,23 @@
     return lax.dot_general(a, b, (((1,), (1,)), ((), ())), preferred_element_type=f32)
 
 
-def owner(h, n_reg):
-    return (h * n_reg) // H
-
-
-def head_of(me, n_reg):
-    h = (me * H + n_reg - 1) // n_reg
-    return jnp.minimum(h, H - 1), jnp.logical_and(h < H, owner(h, n_reg) == me)
+def owner(h, n_reg, mt):
+    base = (h * n_reg) // H
+    if n_reg % 4:
+        return base
+    return base // 4 * 4 + (base + base // 4 + 2 * mt) % 4
+
+
+def head_of(me, n_reg, mt):
+    base = me
+    if n_reg % 4 == 0:
+        base = me // 4 * 4 + (me + 3 * (me // 4) + 2 * mt) % 4
+    h = (base * H + n_reg - 1) // n_reg
+    return jnp.minimum(h, H - 1), jnp.logical_and(h < H, (h * n_reg) // H == base)
 
 
 def peer(me, step, n):
-    if n & (n - 1):
-        return lax.rem(me + step, n)
-    out = me
-    for b in range(n.bit_length() - 1):
-        if step >> b & 1:
-            w = 1 << b
-            out = out + w * (1 - 2 * ((me // w) % 2))
-    return out
+    return lax.rem(me + step, n)
 
 
 def caps_of(n):
@@ -66,7 +65,7 @@
     hd = d // H
     barrier = pltpu.get_barrier_semaphore()
     others = [
-        (k, c) for k in reversed(range(n_reg)) for c in range(n_tm) if (k, c) != (0, 0)
+        (k, c) for k in range(n_reg) for c in range(n_tm) if (k, c) != (0, 0)
     ]
 
     def place(k, c):
@@ -89,7 +88,7 @@
     ]
     for load in loads:
         load.start()
-    head, is_head = head_of(me, n_reg)
+    head, is_head = head_of(me, n_reg, mt)
 
     count = cnt_ref[0, 0]
     csend[...] = jnp.zeros(csend.shape, i32) + count
@@ -142,7 +141,7 @@
         target = peer(me, k, n_reg)
         half, rows = parts[i]
         return pltpu.make_async_remote_copy(
-            src_ref=send.at[head_of(target, n_reg)[0], half, rows],
+            src_ref=send.at[head_of(target, n_reg, mt)[0], half, rows],
             dst_ref=out_ref.at[half, me, rows],
             send_sem=ssem.at[i, k],
             recv_sem=rsem.at[i, me],
@@ -151,9 +150,9 @@
         )
 
     def each(act):
-        for k in reversed(range(1, n_reg)):
-
-            @pl.when(head_of(peer(me, k, n_reg), n_reg)[1])
+        for k in range(1, n_reg):
+
+            @pl.when(head_of(peer(me, k, n_reg), n_reg, mt)[1])
             def _():
                 act(k)
 
@@ -167,9 +166,9 @@
             device_id_type=MESH,
         )
 
-    each(lambda k: away(k, 0).start())
     for j in range(len(others)):
         tell(j).start()
+    each(lambda k: away(k, 0).start())
     loads[4].wait()
     put(dot(hidden, wbuf[2]).astype(bf16), t, 0, 0)
     loads[5].wait()
@@ -267,13 +266,13 @@
     supers = blocks // subs
     step = BLK // PAGE
     barrier = pltpu.get_barrier_semaphore()
-    head, is_head = head_of(me, n_reg)
+    head, is_head = head_of(me, n_reg, mt)
 
     def each(act):
-        for k in reversed(range(1, n_reg)):
+        for k in range(1, n_reg):
             r = peer(me, k, n_reg)
 
-            @pl.when(head_of(r, n_reg)[1])
+            @pl.when(head_of(r, n_reg, mt)[1])
             def _():
                 act(r)
 
@@ -410,7 +409,7 @@
 
     @pl.when(is_head)
     def _():
-        for k in reversed(range(n_reg)):
+        for k in list(range(1, n_reg)) + [0]:
             r = peer(me, k, n_reg)
             begin = tbl_ref[2, r]
             live = lax.broadcasted_iota(i32, (t, width), 0) < tbl_ref[3, r]
@@ -431,7 +430,7 @@
 
     for h in range(H):
 
-        @pl.when(owner(h, n_reg) != me)
+        @pl.when(owner(h, n_reg, mt) != me)
         def _():
             pltpu.make_async_copy(part.at[0], got.at[h], rsem.at[h]).wait()
 

time: 62.3 us -> 57.5 us (0.923)
  the two profiles are of different devices: /device:TPU:0 before, /device:TPU:14 now
where the time goes in v2:
time: 57.5 us; the launch traced here: 56.9 us
  Pallas kernels  53.7 us (93%)
  local copies, waits for them, and re-layouts  1.63 us (3%)
  between operations  1.35 us (2%)
    pallas_call x1, Pallas kernels, shards(): lax.switch(pick[0, 0], [work(i, cap) for i, cap in enumerate(caps)], chun...  27.4 us
    pallas_call x1, Pallas kernels, shards(): pl.pallas_call(functools.partial(spread_kernel, n_reg, n_tm, caps), out_s...  26.2 us
    unnamed x9, local copies, waits for them, and re-layouts  1.63 us

profile of v2, /device:TPU:14, one launch (start us, length us, event | category | flops | bytes accessed | tf_op | source)
XLA Modules:
  0.0 56.9 jit_solution(1856699222834704600)
XLA Ops:
  0.7 0.0 copy-start
  0.7 0.0 copy-start.1
  0.7 0.0 copy-start.2
  0.7 0.0 copy-start.3
  0.7 26.2 %spread.1 = (bf16[2,16,8,16,128]{4,3,2,1,0:T(8,128)(2,1)}, s32[4,128]{1,0:T(4,128)S(1)}, s32[1,1]{1,0:T(1,128)}) custom-call(bf16[1,128,768]{2,1,0:T(8,128)(2,1)} %lat_ref.1, bf16[1,128,768]{2,1,0:T(8,128)(2,1)} %og_ref.1, f32[4,768]{1,0:T(4,128)} %ck_ref.1, s32[1,1]{1,0:T(1,128)S(6)} %copy.16.cnt_ref, bf16[768,768]{1,0:T(8,128)(2,1)} %wq_ref.1, ...), custom_call_target="tpu_custom_call" | custom-call | tf_op jit(solution)/shard_map/spread/pallas_call | solution.py:490
  27.6 0.0 copy-done
  27.6 0.0 copy-done.1
  27.6 0.0 copy-done.2
  27.6 0.0 copy-done.3
  27.6 27.7 %conditional.1 = (bf16[1,128,768]{2,1,0:T(8,128)(2,1)}) conditional(s32[]{:T(128)} %bitcast, (bf16[2,128,16,128]{3,2,1,0:T(8,128)(2,1)}, s32[4,128]{1,0:T(4,128)S(1)}, f32[4,768]{1,0:T(4,128)S(1)}, bf16[768,768]{1,0:T(8,128)(2,1)S(1)}, bf16[768,768]{1,0:T(8,128)(2,1)S(1)}, /*index=5*/bf16[768,768]{1,0:T(8,128)(2,1)S(1)}) %tuple.33, ...), branch_computations={%region_0.0_spmd, %region_1.0_spmd, %region_2.0_spmd} | conditional | bytes 8 | solution.py:554
  27.6 27.4 %work1024.1 = bf16[1,128,768]{2,1,0:T(8,128)(2,1)} custom-call(bf16[2,128,16,128]{3,2,1,0:T(8,128)(2,1)} %get-tuple-element.44.chunk_ref, s32[4,128]{1,0:T(4,128)S(1)} %get-tuple-element.46.tbl_ref, f32[4,768]{1,0:T(4,128)S(1)} %get-tuple-element.47.ck_ref, bf16[768,768]{1,0:T(8,128)(2,1)S(1)} %get-tuple-element.48.wq_ref, ...), custom_call_target="tpu_custom_call" | custom-call | tf_op jit(solution)/shard_map/cond/branch_0_fun/work1024/pallas_call | solution.py:554
  55.3 1.6 %copy.17 = bf16[1,128,768]{2,1,0:T(8,128)(2,1)} copy(bf16[1,128,768]{2,1,0:T(8,128)(2,1)} %get-tuple-element.69) | data formatting | bytes 393216
Async XLA Ops:
  0.7 26.9 %copy-start = (bf16[768,768]{1,0:T(8,128)(2,1)S(1)}, bf16[768,768]{1,0:T(8,128)(2,1)}, u32[]{:S(2)}) copy-start(bf16[768,768]{1,0:T(8,128)(2,1)} %wq_ref.1) | copy-start | bytes 3538948
  0.7 26.9 %copy-start.1 = (bf16[768,768]{1,0:T(8,128)(2,1)S(1)}, bf16[768,768]{1,0:T(8,128)(2,1)}, u32[]{:S(2)}) copy-start(bf16[768,768]{1,0:T(8,128)(2,1)} %wk_ref.1) | copy-start | bytes 3538948
  0.7 26.9 %copy-start.2 = (bf16[768,768]{1,0:T(8,128)(2,1)S(1)}, bf16[768,768]{1,0:T(8,128)(2,1)}, u32[]{:S(2)}) copy-start(bf16[768,768]{1,0:T(8,128)(2,1)} %wv_ref.1) | copy-start | bytes 3538948
  0.7 26.9 %copy-start.3 = (f32[4,768]{1,0:T(4,128)S(1)}, f32[4,768]{1,0:T(4,128)}, u32[]{:S(2)}) copy-start(f32[4,768]{1,0:T(4,128)} %ck_ref.1) | copy-start | bytes 36868

commit v3 on v2

--- a/solution.py
+++ b/solution.py
@@ -13,6 +13,10 @@
 BLK = 256
 PAGE = 16
 CAPS = (1024, 1280)
+GROUP = 4
+SPREAD_VMEM = 20 << 20
+WORK_VMEM = 40 << 20
+FINISH_VMEM = 8 << 20
 NEG = -1e30
 bf16 = jnp.bfloat16
 f32 = jnp.float32
@@ -20,6 +24,7 @@
 VM = pl.BlockSpec(memory_space=pltpu.VMEM)
 SM = pl.BlockSpec(memory_space=pltpu.SMEM)
 ANY = pl.BlockSpec(memory_space=pl.ANY)
+HBM = pl.BlockSpec(memory_space=pltpu.MemorySpace.HBM)
 MESH = pl.DeviceIdType.MESH
 
 
@@ -50,14 +55,18 @@
     return lax.rem(me + step, n)
 
 
+def far(x):
+    return pltpu.with_memory_space_constraint(x, pltpu.MemorySpace.HBM)
+
+
 def caps_of(n):
     return [c for c in CAPS if c < n] + [-(-n // 1024) * 1024]
 
 
 def spread_kernel(
-    n_reg, n_tm, caps, lat_ref, og_ref, ck_ref, cnt_ref, wq_ref, wk_ref, wv_ref, wo_ref,
+    n_reg, n_tm, caps, lat_ref, og_ref, taps_ref, cnt_ref, wq_ref, wk_ref, wv_ref, wo_ref,
     out_ref, table_ref, pick_ref,
-    wbuf, lat, og, ext, edge, send, csend, cbuf, wsem, esem, ssem, rsem, tsem, lsem,
+    ck_ref, wbuf, lat, og, ext, edge, send, csend, cbuf, wsem, esem, ssem, rsem, tsem, lsem,
 ):
     me = lax.axis_index("region")
     mt = lax.axis_index("tm")
@@ -83,6 +92,7 @@
                 (wv_ref, wbuf.at[1]),
                 (wq_ref, wbuf.at[2]),
                 (wk_ref, wbuf.at[3]),
+                (taps_ref, ck_ref),
             )
         )
     ]
@@ -106,6 +116,7 @@
             send[h, half, 0 : rows // PAGE, :, first : first + hd] = part
 
     loads[0].wait()
+    loads[6].wait()
     ext[0:8, :] = jnp.zeros((8, d), f32)
     ext[8 : 8 + t, :] = lat[...].astype(f32)
     hidden = hide(t)
@@ -250,14 +261,14 @@
 
 
 def work_kernel(
-    n_reg, n_tm, cap, chunk_ref, tbl_ref, ck_ref, wq_ref, wk_ref, wv_ref,
-    out_ref,
-    chunk, qk, ka, vg, kt, qt, gt, qg, sbuf, wbuf, dkv, dqp, part,
-    got, wts, xs, ext, wsem, esem, ssem, rsem, lsem,
+    n_reg, n_tm, cap, chunk, tbl_ref, wq_ref, wk_ref, wv_ref,
+    ext_ref,
+    qk, ka, vg, kt, qt, gt, qg, sbuf, wbuf, dkv, dqp, part,
+    got, xs, esem, ssem, rsem, lsem,
 ):
     me = lax.axis_index("region")
     mt = lax.axis_index("tm")
-    t, d = out_ref.shape[1], out_ref.shape[2]
+    t, d = ext_ref.shape[0] - 8, ext_ref.shape[1]
     hd = d // H
     width = 2 * hd
     inv_root = 1.0 / math.sqrt(hd)
@@ -287,18 +298,6 @@
         up = {"tm": jnp.minimum(mt + 1, n_tm - 1)}
         pl.semaphore_signal(barrier, inc=1, device_id=up, device_id_type=MESH)
 
-    fetch = pltpu.make_async_copy(chunk_ref, chunk, lsem.at[1])
-
-    @pl.when(is_head)
-    def _():
-        fetch.start()
-
-    loads = [
-        pltpu.make_async_copy(ref, wts.at[i], wsem.at[i])
-        for i, ref in enumerate((wq_ref, wk_ref, wv_ref))
-    ]
-    for load in loads:
-        load.start()
     peers = jnp.where(is_head, n_reg - 1, 0) + jnp.minimum(mt, 1)
 
     def lane(rows):
@@ -318,8 +317,6 @@
 
     @pl.when(is_head)
     def _():
-        fetch.wait()
-
         def pack(p, c):
             source = tbl_ref[0, p]
             rows = tbl_ref[1, p]
@@ -428,26 +425,34 @@
                 here.start()
         here.wait()
 
-    for h in range(H):
-
-        @pl.when(owner(h, n_reg, mt) != me)
-        def _():
-            pltpu.make_async_copy(part.at[0], got.at[h], rsem.at[h]).wait()
-
-    for h in range(H):
-        cols = slice(h * hd, (h + 1) * hd)
-        xs[0, 0 : t // 2, cols] = got[h, t:, 0:hd]
-        xs[0, t // 2 :, cols] = got[h, t:, hd:]
-        xs[1, :, cols] = got[h, 0:t, 0:hd]
-        xs[2, :, cols] = got[h, 0:t, hd:]
-    for load in loads:
-        load.wait()
-    side = dot_t(xs[1], wts[1]) + dot_t(xs[2], wts[2])
-    ext[0:t, :] = dot_t(xs[0], wts[0]) + side
+    wide = GROUP * hd
+    groups = H // GROUP
+    for j in range(groups):
+        g = jnp.where(2 * me < n_reg, j, groups - 1 - j)
+        for i in range(GROUP):
+            h = g * GROUP + i
+
+            @pl.when(owner(h, n_reg, mt) != me)
+            def _():
+                pltpu.make_async_copy(part.at[0], got.at[h], rsem.at[h]).wait()
+
+            cols = slice(i * hd, (i + 1) * hd)
+            xs[0, 0 : t // 2, cols] = got[h, t:, 0:hd]
+            xs[0, t // 2 :, cols] = got[h, t:, hd:]
+            xs[1, :, cols] = got[h, 0:t, 0:hd]
+            xs[2, :, cols] = got[h, 0:t, hd:]
+        cols = pl.ds(pl.multiple_of(g * wide, wide), wide)
+        add = dot_t(xs[0], wq_ref[:, cols]) + (
+            dot_t(xs[1], wk_ref[:, cols]) + dot_t(xs[2], wv_ref[:, cols])
+        )
+        if j == 0:
+            ext_ref[0:t, :] = add
+        else:
+            ext_ref[0:t, :] += add
 
     to_prev = pltpu.make_async_remote_copy(
-        src_ref=ext.at[pl.ds(0, 8)],
-        dst_ref=ext.at[pl.ds(t, 8)],
+        src_ref=ext_ref.at[pl.ds(0, 8)],
+        dst_ref=ext_ref.at[pl.ds(t, 8)],
         send_sem=esem.at[0],
         recv_sem=esem.at[1],
         device_id={"tm": jnp.maximum(mt - 1, 0)},
@@ -465,20 +470,23 @@
 
     @pl.when(mt == n_tm - 1)
     def _():
-        ext[t : t + 8, :] = jnp.zeros((8, d), f32)
+        ext_ref[t : t + 8, :] = jnp.zeros((8, d), f32)
 
     @pl.when(mt < n_tm - 1)
     def _():
         to_prev.wait_recv()
 
-    total = ck_ref[0:1, :] * ext[0:t, :]
+    @pl.when(mt > 0)
+    def _():
+        to_prev.wait_send()
+
+
+def finish_kernel(ext_ref, ck_ref, out_ref):
+    t = out_ref.shape[1]
+    total = ck_ref[0:1, :] * ext_ref[0:t, :]
     for j in range(1, KW):
-        total = total + ck_ref[j : j + 1, :] * ext[j : j + t, :]
+        total = total + ck_ref[j : j + 1, :] * ext_ref[j : j + t, :]
     out_ref[0] = total.astype(bf16)
-
-    @pl.when(mt > 0)
-    def _():
-        to_prev.wait_send()
 
 
 def shards(n_reg, n_tm, latents, output_grad, conv_kernel, w_query, w_key, w_value, w_out, live_counts):
@@ -494,9 +502,10 @@
             jax.ShapeDtypeStruct((4, lanes), i32),
             jax.ShapeDtypeStruct((1, 1), i32),
         ),
-        in_specs=[ANY, ANY, VM, SM, ANY, ANY, ANY, ANY],
+        in_specs=[HBM, HBM, HBM, SM, HBM, HBM, HBM, HBM],
         out_specs=(ANY, VM, SM),
         scratch_shapes=[
+            pltpu.VMEM(conv_kernel.shape, f32),
             pltpu.VMEM((4, d, d), bf16),
             pltpu.VMEM((t, d), bf16),
             pltpu.VMEM((t, d), bf16),
@@ -505,26 +514,27 @@
             pltpu.VMEM((H, 2, t // PAGE, PAGE, 2 * hd), bf16),
             pltpu.VMEM((1, lanes), i32),
             pltpu.VMEM((n_tm, n_reg, 1, lanes), i32),
-            dma((6,)),
+            dma((7,)),
             dma((2,)),
             dma((3, n_reg)),
             dma((3, n_reg)),
             dma((2, n_reg * n_tm)),
             dma((1,)),
         ],
-        compiler_params=pltpu.CompilerParams(collective_id=0, has_side_effects=True),
+        compiler_params=pltpu.CompilerParams(
+            collective_id=0, has_side_effects=True, vmem_limit_bytes=SPREAD_VMEM
+        ),
         name="spread",
-    )(latents, output_grad, conv_kernel, live_counts, w_query, w_key, w_value, w_out)
+    )(far(latents), far(output_grad), far(conv_kernel), live_counts, far(w_query), far(w_key), far(w_value), far(w_out))
 
     def work(i, cap):
         blocks = cap // BLK
         return pl.pallas_call(
             functools.partial(work_kernel, n_reg, n_tm, cap),
-            out_shape=jax.ShapeDtypeStruct((1, t, d), bf16),
-            in_specs=[ANY, SM, VM, ANY, ANY, ANY],
+            out_shape=jax.ShapeDtypeStruct((t + 8, d), f32),
+            in_specs=[VM, SM, VM, VM, VM],
             out_specs=VM,
             scratch_shapes=[
-                pltpu.VMEM((2, n_reg * t // PAGE, PAGE, 2 * hd), bf16),
                 pltpu.VMEM((cap, 2 * hd), bf16),
                 pltpu.VMEM((cap, 2 * hd), bf16),
                 pltpu.VMEM((cap, 2 * hd), bf16),
@@ -538,24 +548,31 @@
                 pltpu.VMEM(((cap + t) // PAGE, PAGE, 2 * hd), f32),
                 pltpu.VMEM((n_reg, t + t // 2, 2 * hd), bf16),
                 pltpu.VMEM((H, t + t // 2, 2 * hd), bf16),
-                pltpu.VMEM((3, d, d), bf16),
-                pltpu.VMEM((3, t, d), bf16),
-                pltpu.VMEM((t + 8, d), f32),
-                dma((3,)),
+                pltpu.VMEM((3, t, GROUP * hd), bf16),
                 dma((2,)),
                 dma((n_reg,)),
                 dma((H,)),
-                dma((2,)),
+                dma((1,)),
             ],
-            compiler_params=pltpu.CompilerParams(collective_id=i + 1, has_side_effects=True),
+            compiler_params=pltpu.CompilerParams(
+                collective_id=i + 1, has_side_effects=True, vmem_limit_bytes=WORK_VMEM
+            ),
             name=f"work{cap}",
         )
 
-    return lax.switch(
+    ext = lax.switch(
         pick[0, 0],
         [work(i, cap) for i, cap in enumerate(caps)],
-        chunks.reshape(2, n_reg * t // PAGE, PAGE, 2 * hd), table, conv_kernel, w_query, w_key, w_value,
+        chunks.reshape(2, n_reg * t // PAGE, PAGE, 2 * hd), table, w_query, w_key, w_value,
     )
+    return pl.pallas_call(
+        finish_kernel,
+        out_shape=jax.ShapeDtypeStruct((1, t, d), bf16),
+        in_specs=[VM, VM],
+        out_specs=VM,
+        compiler_params=pltpu.CompilerParams(vmem_limit_bytes=FINISH_VMEM),
+        name="finish",
+    )(ext, conv_kernel)
 
 
 def solution(mesh):

time: 57.5 us -> 55.2 us (0.960); the launches traced: 56.9 us -> 55.6 us
  local copies, waits for them, and re-layouts: 1.63 us -> 0.02 us
    unnamed x9 -> x8, local copies, waits for them, and re-layouts: 1.63 us -> 0.02 us
    pallas_call x0 -> x1, Pallas kernels: none -> 0.9 us  [shards(): pl.pallas_call(finish_kernel, out_shape=jax.ShapeDtypeStruct((1, t, d), b...]
where the time goes in v3:
time: 55.2 us; the launch traced here: 55.6 us
  Pallas kernels  53.9 us (98%)
  between operations  1.41 us (3%)
    pallas_call x1, Pallas kernels, shards(): lax.switch(pick[0, 0], [work(i, cap) for i, cap in enumerate(caps)], chun...  27.1 us
    pallas_call x1, Pallas kernels, shards(): pl.pallas_call(functools.partial(spread_kernel, n_reg, n_tm, caps), out_s...  25.9 us

profile of v3, /device:TPU:14, one launch (start us, length us, event | category | flops | bytes accessed | tf_op | source)
XLA Modules:
  0.0 55.6 jit_solution(8783538071536023475)
XLA Ops:
  0.7 0.0 copy-start.1
  0.7 0.0 copy-start.2
  0.7 0.0 copy-start.3
  0.7 25.9 %spread.1 = (bf16[2,16,8,16,128]{4,3,2,1,0:T(8,128)(2,1)S(1)}, s32[4,128]{1,0:T(4,128)S(1)}, s32[1,1]{1,0:T(1,128)}) custom-call(bf16[1,128,768]{2,1,0:T(8,128)(2,1)} %lat_ref.1, bf16[1,128,768]{2,1,0:T(8,128)(2,1)} %og_ref.1, f32[4,768]{1,0:T(4,128)} %ck_ref.1, s32[1,1]{1,0:T(1,128)S(6)} %copy.12.cnt_ref, bf16[768,768]{1,0:T(8,128)(2,1)} %wq_ref.1, ...), custom_call_target="tpu_custom_call" | custom-call | tf_op jit(solution)/shard_map/spread/pallas_call | solution.py:498
  27.3 0.0 copy-done.1
  27.3 0.0 copy-done.2
  27.3 0.0 copy-done.3
  27.3 0.0 copy-start
  27.3 27.3 %conditional.1 = (f32[136,768]{1,0:T(8,128)S(1)}) conditional(s32[]{:T(128)} %bitcast, (bf16[2,128,16,128]{3,2,1,0:T(8,128)(2,1)S(1)}, s32[4,128]{1,0:T(4,128)S(1)}, bf16[768,768]{1,0:T(8,128)(2,1)S(1)}, bf16[768,768]{1,0:T(8,128)(2,1)S(1)}, bf16[768,768]{1,0:T(8,128)(2,1)S(1)}) %tuple.27, (bf16[2,128,16,128]{3,2,1,0:T(8,128)(2,1)S(1)}, ...), branch_computations={%region_0.0_spmd, %region_1.0_spmd, %region_2.0_spmd} | conditional | bytes 8 | solution.py:563
  27.3 27.1 %work1280.1 = f32[136,768]{1,0:T(8,128)S(1)} custom-call(bf16[2,128,16,128]{3,2,1,0:T(8,128)(2,1)S(1)} %get-tuple-element.44.chunk, s32[4,128]{1,0:T(4,128)S(1)} %get-tuple-element.45.tbl_ref, bf16[768,768]{1,0:T(8,128)(2,1)S(1)} %get-tuple-element.46.wq_ref, bf16[768,768]{1,0:T(8,128)(2,1)S(1)} %get-tuple-element.47.wk_ref, ...), custom_call_target="tpu_custom_call" | custom-call | tf_op jit(solution)/shard_map/cond/branch_1_fun/work1280/pallas_call | solution.py:563
  54.7 0.0 copy-done
  54.7 0.9 %finish.1 = bf16[1,128,768]{2,1,0:T(8,128)(2,1)} custom-call(f32[136,768]{1,0:T(8,128)S(1)} %get-tuple-element.60.ext_ref, f32[4,768]{1,0:T(4,128)S(1)} %copy-done), custom_call_target="tpu_custom_call" | custom-call | tf_op jit(solution)/shard_map/finish/pallas_call | solution.py:568
Async XLA Ops:
  0.7 26.6 %copy-start.1 = (bf16[768,768]{1,0:T(8,128)(2,1)S(1)}, bf16[768,768]{1,0:T(8,128)(2,1)}, u32[]{:S(2)}) copy-start(bf16[768,768]{1,0:T(8,128)(2,1)} %wq_ref.1) | copy-start | bytes 3538948
  0.7 26.6 %copy-start.2 = (bf16[768,768]{1,0:T(8,128)(2,1)S(1)}, bf16[768,768]{1,0:T(8,128)(2,1)}, u32[]{:S(2)}) copy-start(bf16[768,768]{1,0:T(8,128)(2,1)} %wk_ref.1) | copy-start | bytes 3538948
  0.7 26.6 %copy-start.3 = (bf16[768,768]{1,0:T(8,128)(2,1)S(1)}, bf16[768,768]{1,0:T(8,128)(2,1)}, u32[]{:S(2)}) copy-start(bf16[768,768]{1,0:T(8,128)(2,1)} %wv_ref.1) | copy-start | bytes 3538948
  27.3 27.4 %copy-start = (f32[4,768]{1,0:T(4,128)S(1)}, f32[4,768]{1,0:T(4,128)}, u32[]{:S(2)}) copy-start(f32[4,768]{1,0:T(4,128)} %ck_ref.1) | copy-start | bytes 36868
